TPU v7x, 32 devices: a whole 2x2x4 slice. The times are simulated.
32 devices in a mesh: section: 2 (over y), expert: 16 (over z, x, core).
Axes of the slice: x: 2, y: 2, z: 4, core: 2. Of those that a mesh axis runs over, the one named last changes fastest.
Arguments:
- inputs: bfloat16 [2, 256, 2560], P('section', 'expert'), may hold values from -6 to 6
- norm_gain: float32 [2, 2, 2560], P(None, 'section'), may hold values from 0.5 to 1.5
- router: bfloat16 [2, 2, 2560, 16], P(None, 'section'), may hold values from -0.125 to 0.125
- w_gate: bfloat16 [2, 2, 16, 2560, 768], P(None, 'section', 'expert'), may hold values from -0.125 to 0.125
- w_up: bfloat16 [2, 2, 16, 2560, 768], P(None, 'section', 'expert'), may hold values from -0.125 to 0.125
- w_down: bfloat16 [2, 2, 16, 768, 2560], P(None, 'section', 'expert'), may hold values from -0.21875 to 0.21875
- routes: int32 [2, 2, 2, 256, 6], P(None, 'section'), may hold values from 0 to 15, all different within a row; in each aligned block of 16 rows (0 to 15, 16 to 31, ..., all dimensions but the last counted through in order) at most 9 rows name the same one
Outputs:
- outputs: bfloat16 [2, 256, 2560], P('section', 'expert')
Inputs may be any that keep to these rules, and one draw needn't show every extreme that they name: Each row names 6 different experts. In each aligned block of 16 rows of routes (the tokens of one index of expert in one micro-batch at one layer), no expert is named by more than 9 rows.
All inputs are finite; a program needn't handle non-finite values.
Results may differ from a plain program's by a relative error of at most 0.012.
Values may be sent and summed in bfloat16 or wider, within the bound.
A program may use at most 64 MiB of HBM per device.

v0:
```python
import jax
import jax.numpy as jnp
from jax import lax
from jax.sharding import PartitionSpec as P


def passed_along(array, axis, by):
    size = lax.axis_size(axis)
    return lax.ppermute(array, axis, [(i, (i + by) % size) for i in range(size)])


def passed_along_2(block, axis, distance):
    devices = range(lax.axis_size(axis))
    route = [(i - distance, i) for i in devices if i - distance in devices]
    return lax.ppermute(block, axis, route)


def normalize(values, gain_row):
    wide = values.astype(jnp.float32)
    scale = lax.rsqrt(jnp.mean(wide * wide, axis=-1, keepdims=True) + 1e-06)
    return (wide * scale * gain_row).astype(jnp.bfloat16)


def gate_weights(normed, router_now, routes_rows):
    scores = jnp.dot(normed, router_now, preferred_element_type=jnp.float32)
    expert_ids = lax.broadcasted_iota(jnp.int32, (1, 1, router_now.shape[1]), 2)
    onehot = (routes_rows[:, :, None] == expert_ids).astype(jnp.float32)
    picked = jnp.sum(onehot * scores[:, None, :], axis=2)
    sigmoid_of = jax.nn.sigmoid(picked)
    return sigmoid_of / jnp.sum(sigmoid_of, axis=1, keepdims=True)


def slot_table(routes_rows, slab_rows, experts):
    top_k = routes_rows.shape[1]
    blocks = routes_rows.reshape(-1, slab_rows * top_k)
    expert_ids = lax.broadcasted_iota(jnp.int32, (1, 1, experts), 2)
    onehot = (blocks[:, :, None] == expert_ids).astype(jnp.int32)
    before = jnp.cumsum(onehot, axis=1) - onehot
    return jnp.sum(before * onehot, axis=2).reshape(routes_rows.shape)


def expert_rows(rows_in, gate_mat, up_mat, down_mat):
    gate_proj = jnp.dot(rows_in, gate_mat, preferred_element_type=jnp.float32)
    up_proj = jnp.dot(rows_in, up_mat, preferred_element_type=jnp.float32)
    hidden = (jax.nn.silu(gate_proj) * up_proj).astype(jnp.bfloat16)
    return jnp.dot(hidden, down_mat, preferred_element_type=jnp.float32).astype(jnp.bfloat16)


def weighted_rows(weights, values):
    upper = weights.astype(jnp.bfloat16)
    lower = (weights - upper.astype(jnp.float32)).astype(jnp.bfloat16)
    first = jnp.dot(upper, values, preferred_element_type=jnp.float32)
    return first + jnp.dot(lower, values, preferred_element_type=jnp.float32)


def per_device(inputs, norm_gain, router, w_gate, w_up, w_down, routes):
    sections = lax.axis_size("section")
    section_at = lax.axis_index("section")
    owner_at = lax.axis_index("expert")
    slab_rows = inputs.shape[1]
    feature = inputs.shape[2]
    experts = router.shape[3]
    top_k = routes.shape[4]
    capacity = min(slab_rows, 3 * slab_rows * top_k // (2 * experts))
    step_count = 3 * sections - 1
    positions = lax.broadcasted_iota(jnp.int32, (1, 1, experts * capacity), 2)

    def layer(slab_in, moment):
        offset = moment - section_at
        is_busy = (offset >= 0) & (offset < 2 * sections)
        clipped = jnp.clip(offset, 0, 2 * sections - 1)
        loop_at = clipped // sections
        micro_at = clipped % sections
        gain_row = lax.dynamic_index_in_dim(norm_gain[:, 0], loop_at, 0, keepdims=False)
        router_now = lax.dynamic_index_in_dim(router[:, 0], loop_at, 0, keepdims=False)
        gate_mat = lax.dynamic_index_in_dim(w_gate[:, 0, 0], loop_at, 0, keepdims=False)
        up_mat = lax.dynamic_index_in_dim(w_up[:, 0, 0], loop_at, 0, keepdims=False)
        down_mat = lax.dynamic_index_in_dim(w_down[:, 0, 0], loop_at, 0, keepdims=False)
        routes_loop = lax.dynamic_index_in_dim(routes[:, 0], loop_at, 0, keepdims=False)
        routes_now = lax.dynamic_index_in_dim(routes_loop, micro_at, 0, keepdims=False)
        normed = normalize(slab_in, gain_row)
        own_routes = lax.dynamic_slice_in_dim(routes_now, owner_at * slab_rows, slab_rows, 0)
        gates = gate_weights(normed, router_now, own_routes)
        slots = slot_table(own_routes, slab_rows, experts)
        placed = own_routes * capacity + slots
        matches = placed[:, :, None] == positions
        select = jnp.any(matches, axis=1).astype(jnp.bfloat16)
        combine = jnp.sum(jnp.where(matches, gates[:, :, None], 0.0), axis=1)
        sending = jnp.einsum(
            "rp,rd->pd", select, normed, preferred_element_type=jnp.float32
        ).astype(jnp.bfloat16)
        sending = sending.reshape(experts, capacity, feature)
        received = lax.all_to_all(sending, "expert", split_axis=0, concat_axis=0, tiled=True)
        answered = lax.cond(
            is_busy,
            lambda values: expert_rows(values, gate_mat, up_mat, down_mat),
            jnp.zeros_like,
            received.reshape(-1, feature),
        ).reshape(received.shape)
        returned = lax.all_to_all(answered, "expert", split_axis=0, concat_axis=0, tiled=True)
        mixed = weighted_rows(combine, returned.reshape(-1, feature))
        return ((slab_in.astype(jnp.float32) + mixed).astype(jnp.bfloat16), micro_at)

    empty_slab = jnp.zeros_like(inputs[0])
    initial = (empty_slab, inputs[0], empty_slab)

    def advance(moment, loop_state):
        carried, feed_box, outbox = loop_state
        entering = (section_at == 0) & (moment < sections)
        fresh = feed_box
        slab_in = jnp.where(entering, fresh, carried)
        result, micro_at = layer(slab_in, moment)
        carried = passed_along(result, "section", 1)
        finish = (section_at == sections - 1) & (moment >= 2 * sections - 1)
        feed_box, outbox = passed_along_2((feed_box, outbox), "section", -1)
        outbox = jnp.where(finish, result, outbox)
        return (carried, feed_box, outbox)

    loop_state = lax.fori_loop(0, step_count, advance, initial)
    return loop_state[2][None]


def solution(mesh):
    return jax.shard_map(
        per_device,
        mesh=mesh,
        in_specs=(
            P("section", "expert", None),
            P(None, "section", None),
            P(None, "section", None, None),
            P(None, "section", "expert", None, None),
            P(None, "section", "expert", None, None),
            P(None, "section", "expert", None, None),
            P(None, "section", None, None, None),
        ),
        out_specs=P("section", "expert", None),
        check_vma=False,
    )
```

profile of v0, /device:TPU:20, one launch (start us, length us, event | category | flops | bytes accessed | tf_op | source)
XLA Modules:
  0.0 453.2 jit_solution(15295944289878618531)
XLA Ops:
  0.9 451.7 %while.21 = (s32[]{:T(128)}, bf16[16,2560]{1,0:T(8,128)(2,1)S(1)}, bf16[16,2560]{1,0:T(8,128)(2,1)S(1)}, bf16[16,2560]{1,0:T(8,128)(2,1)S(1)}, pred[]{:T(512)}, ...) while((s32[]{:T(128)}, bf16[16,2560]{1,0:T(8,128)(2,1)S(1)}, ...), condition=%wide.region_10.11_spmd.clone, body=%wide.region_0.10_spmd.clone.sunk | while | flops 1737769472 | bytes 32948616 | solution.py:119
  5.3 6.2 %all-to-all-start = ((bf16[16,9,2560]{2,1,0:T(8,128)(2,1)}), bf16[16,9,2560]{2,1,0:T(8,128)(2,1)S(1)}, u32[]{:S(2)}, u32[]{:S(2)}) async-start(bf16[16,9,2560]{2,1,0:T(8,128)(2,1)} %reshape.244), calls=%async_computation | async-start | bytes 2621440 | tf_op jit(solution)/shard_map/while/body/eval_jaxpr/all_to_all | solution.py:93
  11.4 2.4 collective-permute-start.2
  13.8 28.4 %all-to-all-done = bf16[16,9,2560]{2,1,0:T(8,128)(2,1)S(1)} async-done(((bf16[16,9,2560]{2,1,0:T(8,128)(2,1)}), bf16[16,9,2560]{2,1,0:T(8,128)(2,1)S(1)}, u32[]{:S(2)}, u32[]{:S(2)}) %all-to-all-start) | async-done | bytes 737312 | tf_op jit(solution)/shard_map/while/body/eval_jaxpr/all_to_all | solution.py:93
  43.7 4.6 %all-to-all-start.1 = ((bf16[16,9,2560]{2,1,0:T(8,128)(2,1)}), bf16[16,9,2560]{2,1,0:T(8,128)(2,1)S(1)}, u32[]{:S(2)}, u32[]{:S(2)}) async-start(bf16[16,9,2560]{2,1,0:T(8,128)(2,1)} %reshape.245), calls=%async_computation.1 | async-start | bytes 2621440 | tf_op jit(solution)/shard_map/while/body/eval_jaxpr/all_to_all | solution.py:100
  48.3 10.6 %collective-permute-start = (bf16[16,2560]{1,0:T(8,128)(2,1)S(1)}, bf16[16,2560]{1,0:T(8,128)(2,1)S(1)}, u32[]{:S(2)}, u32[]{:S(2)}) collective-permute-start(bf16[16,2560]{1,0:T(8,128)(2,1)S(1)} %broadcast_select_fusion.6), channel_id=1, source_target_pairs={{16,0},{17,1},{18,2},{19,3},{20,4},{21,5},{22,6},{23,7},{24,8},{25... | collective-permute-start | bytes 245768 | tf_op jit(solution)/shard_map/while/body/eval_jaxpr/ppermute | solution.py:15
  59.5 19.6 %all-to-all-done.1 = bf16[16,9,2560]{2,1,0:T(8,128)(2,1)S(1)} async-done(((bf16[16,9,2560]{2,1,0:T(8,128)(2,1)}), bf16[16,9,2560]{2,1,0:T(8,128)(2,1)S(1)}, u32[]{:S(2)}, u32[]{:S(2)}) %all-to-all-start.1) | async-done | bytes 737312 | tf_op jit(solution)/shard_map/while/body/eval_jaxpr/all_to_all | solution.py:100
  79.8 8.8 %collective-permute-start.1 = (bf16[16,2560]{1,0:T(8,128)(2,1)S(1)}, bf16[16,2560]{1,0:T(8,128)(2,1)S(1)}, u32[]{:S(2)}, u32[]{:S(2)}) collective-permute-start(bf16[16,2560]{1,0:T(8,128)(2,1)S(1)} %get-tuple-element.674), channel_id=1, source_target_pairs={{0,16},{16,0},{1,17},{17,1},{2,18},{18,2},{3,19},{19,3},{4,20},{20... | collective-permute-start | bytes 245768 | tf_op jit(solution)/shard_map/while/body/eval_jaxpr/ppermute | solution.py:9
  88.6 2.4 collective-permute-done.1
  95.4 5.1 %all-to-all-start = ((bf16[16,9,2560]{2,1,0:T(8,128)(2,1)}), bf16[16,9,2560]{2,1,0:T(8,128)(2,1)S(1)}, u32[]{:S(2)}, u32[]{:S(2)}) async-start(bf16[16,9,2560]{2,1,0:T(8,128)(2,1)} %reshape.244), calls=%async_computation | async-start | bytes 2621440 | tf_op jit(solution)/shard_map/while/body/eval_jaxpr/all_to_all | solution.py:93
  100.5 3.6 collective-permute-start.2
  104.2 27.1 %all-to-all-done = bf16[16,9,2560]{2,1,0:T(8,128)(2,1)S(1)} async-done(((bf16[16,9,2560]{2,1,0:T(8,128)(2,1)}), bf16[16,9,2560]{2,1,0:T(8,128)(2,1)S(1)}, u32[]{:S(2)}, u32[]{:S(2)}) %all-to-all-start) | async-done | bytes 737312 | tf_op jit(solution)/shard_map/while/body/eval_jaxpr/all_to_all | solution.py:93
  131.3 8.3 %conditional.3 = (bf16[144,2560]{1,0:T(8,128)(2,1)S(1)}) conditional(s32[]{:T(128)} %convert_element_type.207, () %tuple.69, (bf16[2,1,1,2560,768]{4,3,2,1,0:T(8,128)(2,1)}, s32[]{:T(128)}, bf16[16,9,2560]{2,1,0:T(8,128)(2,1)S(1)}, bf16[2,1,1,2560,768]{4,3,2,1,0:T(8,128)(2,1)}, bf16[2,1,1,768,2560]{4,3,2,1,0:T(8,128)(2,1)}) %tuple.70), branch_computations={%region_8.8_spmd, %region_9.9_spmd} | conditional | flops 1699725312 | bytes 16369160 | solution.py:94
  131.6 2.9 fusion.14
  134.5 5.1 %fusion.11 = bf16[144,2560]{1,0:T(8,128)(2,1)S(1)} fusion(bf16[2,1,1,768,2560]{4,3,2,1,0:T(8,128)(2,1)} %get-tuple-element.443, s32[]{:T(128)} %get-tuple-element.440, bf16[144,2560]{1,0:T(8,128)(2,1)S(1)} %reshape.229, bf16[2,1,1,2560,768]{4,3,2,1,0:T(8,128)(2,1)} %get-tuple-element.442, f32[144,768]{1,0:T(8,128)S(1)} %fusion.14), kind=kOutput, calls=%fused_computation.10 | convolution fusion | flops 1133494272 | bytes 9782272 | tf_op jit(solution)/shard_map/while/body/eval_jaxpr/cond/branch_1_fun/dot_general | solution.py:46
  140.9 4.6 %all-to-all-start.1 = ((bf16[16,9,2560]{2,1,0:T(8,128)(2,1)}), bf16[16,9,2560]{2,1,0:T(8,128)(2,1)S(1)}, u32[]{:S(2)}, u32[]{:S(2)}) async-start(bf16[16,9,2560]{2,1,0:T(8,128)(2,1)} %reshape.245), calls=%async_computation.1 | async-start | bytes 2621440 | tf_op jit(solution)/shard_map/while/body/eval_jaxpr/all_to_all | solution.py:100
  145.6 3.7 collective-permute-start
  149.8 26.5 %all-to-all-done.1 = bf16[16,9,2560]{2,1,0:T(8,128)(2,1)S(1)} async-done(((bf16[16,9,2560]{2,1,0:T(8,128)(2,1)}), bf16[16,9,2560]{2,1,0:T(8,128)(2,1)S(1)}, u32[]{:S(2)}, u32[]{:S(2)}) %all-to-all-start.1) | async-done | bytes 737312 | tf_op jit(solution)/shard_map/while/body/eval_jaxpr/all_to_all | solution.py:100
  178.9 2.7 collective-permute-done.1
  186.0 4.8 %all-to-all-start = ((bf16[16,9,2560]{2,1,0:T(8,128)(2,1)}), bf16[16,9,2560]{2,1,0:T(8,128)(2,1)S(1)}, u32[]{:S(2)}, u32[]{:S(2)}) async-start(bf16[16,9,2560]{2,1,0:T(8,128)(2,1)} %reshape.244), calls=%async_computation | async-start | bytes 2621440 | tf_op jit(solution)/shard_map/while/body/eval_jaxpr/all_to_all | solution.py:93
  190.8 3.6 collective-permute-start.2
  194.5 27.1 %all-to-all-done = bf16[16,9,2560]{2,1,0:T(8,128)(2,1)S(1)} async-done(((bf16[16,9,2560]{2,1,0:T(8,128)(2,1)}), bf16[16,9,2560]{2,1,0:T(8,128)(2,1)S(1)}, u32[]{:S(2)}, u32[]{:S(2)}) %all-to-all-start) | async-done | bytes 737312 | tf_op jit(solution)/shard_map/while/body/eval_jaxpr/all_to_all | solution.py:93
  221.6 8.3 %conditional.3 = (bf16[144,2560]{1,0:T(8,128)(2,1)S(1)}) conditional(s32[]{:T(128)} %convert_element_type.207, () %tuple.69, (bf16[2,1,1,2560,768]{4,3,2,1,0:T(8,128)(2,1)}, s32[]{:T(128)}, bf16[16,9,2560]{2,1,0:T(8,128)(2,1)S(1)}, bf16[2,1,1,2560,768]{4,3,2,1,0:T(8,128)(2,1)}, bf16[2,1,1,768,2560]{4,3,2,1,0:T(8,128)(2,1)}) %tuple.70), branch_computations={%region_8.8_spmd, %region_9.9_spmd} | conditional | flops 1699725312 | bytes 16369160 | solution.py:94
  221.9 2.9 fusion.14
  224.8 5.1 %fusion.11 = bf16[144,2560]{1,0:T(8,128)(2,1)S(1)} fusion(bf16[2,1,1,768,2560]{4,3,2,1,0:T(8,128)(2,1)} %get-tuple-element.443, s32[]{:T(128)} %get-tuple-element.440, bf16[144,2560]{1,0:T(8,128)(2,1)S(1)} %reshape.229, bf16[2,1,1,2560,768]{4,3,2,1,0:T(8,128)(2,1)} %get-tuple-element.442, f32[144,768]{1,0:T(8,128)S(1)} %fusion.14), kind=kOutput, calls=%fused_computation.10 | convolution fusion | flops 1133494272 | bytes 9782272 | tf_op jit(solution)/shard_map/while/body/eval_jaxpr/cond/branch_1_fun/dot_general | solution.py:46
  231.3 4.6 %all-to-all-start.1 = ((bf16[16,9,2560]{2,1,0:T(8,128)(2,1)}), bf16[16,9,2560]{2,1,0:T(8,128)(2,1)S(1)}, u32[]{:S(2)}, u32[]{:S(2)}) async-start(bf16[16,9,2560]{2,1,0:T(8,128)(2,1)} %reshape.245), calls=%async_computation.1 | async-start | bytes 2621440 | tf_op jit(solution)/shard_map/while/body/eval_jaxpr/all_to_all | solution.py:100
  235.9 3.7 collective-permute-start
  240.1 26.5 %all-to-all-done.1 = bf16[16,9,2560]{2,1,0:T(8,128)(2,1)S(1)} async-done(((bf16[16,9,2560]{2,1,0:T(8,128)(2,1)}), bf16[16,9,2560]{2,1,0:T(8,128)(2,1)S(1)}, u32[]{:S(2)}, u32[]{:S(2)}) %all-to-all-start.1) | async-done | bytes 737312 | tf_op jit(solution)/shard_map/while/body/eval_jaxpr/all_to_all | solution.py:100
  269.3 2.7 collective-permute-done.1
  276.3 4.8 %all-to-all-start = ((bf16[16,9,2560]{2,1,0:T(8,128)(2,1)}), bf16[16,9,2560]{2,1,0:T(8,128)(2,1)S(1)}, u32[]{:S(2)}, u32[]{:S(2)}) async-start(bf16[16,9,2560]{2,1,0:T(8,128)(2,1)} %reshape.244), calls=%async_computation | async-start | bytes 2621440 | tf_op jit(solution)/shard_map/while/body/eval_jaxpr/all_to_all | solution.py:93
  281.1 3.6 collective-permute-start.2
  284.8 27.1 %all-to-all-done = bf16[16,9,2560]{2,1,0:T(8,128)(2,1)S(1)} async-done(((bf16[16,9,2560]{2,1,0:T(8,128)(2,1)}), bf16[16,9,2560]{2,1,0:T(8,128)(2,1)S(1)}, u32[]{:S(2)}, u32[]{:S(2)}) %all-to-all-start) | async-done | bytes 737312 | tf_op jit(solution)/shard_map/while/body/eval_jaxpr/all_to_all | solution.py:93
  311.9 8.3 %conditional.3 = (bf16[144,2560]{1,0:T(8,128)(2,1)S(1)}) conditional(s32[]{:T(128)} %convert_element_type.207, () %tuple.69, (bf16[2,1,1,2560,768]{4,3,2,1,0:T(8,128)(2,1)}, s32[]{:T(128)}, bf16[16,9,2560]{2,1,0:T(8,128)(2,1)S(1)}, bf16[2,1,1,2560,768]{4,3,2,1,0:T(8,128)(2,1)}, bf16[2,1,1,768,2560]{4,3,2,1,0:T(8,128)(2,1)}) %tuple.70), branch_computations={%region_8.8_spmd, %region_9.9_spmd} | conditional | flops 1699725312 | bytes 16369160 | solution.py:94
  312.2 2.9 fusion.14
  315.1 5.1 %fusion.11 = bf16[144,2560]{1,0:T(8,128)(2,1)S(1)} fusion(bf16[2,1,1,768,2560]{4,3,2,1,0:T(8,128)(2,1)} %get-tuple-element.443, s32[]{:T(128)} %get-tuple-element.440, bf16[144,2560]{1,0:T(8,128)(2,1)S(1)} %reshape.229, bf16[2,1,1,2560,768]{4,3,2,1,0:T(8,128)(2,1)} %get-tuple-element.442, f32[144,768]{1,0:T(8,128)S(1)} %fusion.14), kind=kOutput, calls=%fused_computation.10 | convolution fusion | flops 1133494272 | bytes 9782272 | tf_op jit(solution)/shard_map/while/body/eval_jaxpr/cond/branch_1_fun/dot_general | solution.py:46
  321.6 4.6 %all-to-all-start.1 = ((bf16[16,9,2560]{2,1,0:T(8,128)(2,1)}), bf16[16,9,2560]{2,1,0:T(8,128)(2,1)S(1)}, u32[]{:S(2)}, u32[]{:S(2)}) async-start(bf16[16,9,2560]{2,1,0:T(8,128)(2,1)} %reshape.245), calls=%async_computation.1 | async-start | bytes 2621440 | tf_op jit(solution)/shard_map/while/body/eval_jaxpr/all_to_all | solution.py:100
  326.2 3.7 collective-permute-start
  330.5 26.5 %all-to-all-done.1 = bf16[16,9,2560]{2,1,0:T(8,128)(2,1)S(1)} async-done(((bf16[16,9,2560]{2,1,0:T(8,128)(2,1)}), bf16[16,9,2560]{2,1,0:T(8,128)(2,1)S(1)}, u32[]{:S(2)}, u32[]{:S(2)}) %all-to-all-start.1) | async-done | bytes 737312 | tf_op jit(solution)/shard_map/while/body/eval_jaxpr/all_to_all | solution.py:100
  359.6 2.7 collective-permute-done.1
  366.6 4.8 %all-to-all-start = ((bf16[16,9,2560]{2,1,0:T(8,128)(2,1)}), bf16[16,9,2560]{2,1,0:T(8,128)(2,1)S(1)}, u32[]{:S(2)}, u32[]{:S(2)}) async-start(bf16[16,9,2560]{2,1,0:T(8,128)(2,1)} %reshape.244), calls=%async_computation | async-start | bytes 2621440 | tf_op jit(solution)/shard_map/while/body/eval_jaxpr/all_to_all | solution.py:93
  371.4 3.6 collective-permute-start.2
  375.1 27.1 %all-to-all-done = bf16[16,9,2560]{2,1,0:T(8,128)(2,1)S(1)} async-done(((bf16[16,9,2560]{2,1,0:T(8,128)(2,1)}), bf16[16,9,2560]{2,1,0:T(8,128)(2,1)S(1)}, u32[]{:S(2)}, u32[]{:S(2)}) %all-to-all-start) | async-done | bytes 737312 | tf_op jit(solution)/shard_map/while/body/eval_jaxpr/all_to_all | solution.py:93
  402.2 8.3 %conditional.3 = (bf16[144,2560]{1,0:T(8,128)(2,1)S(1)}) conditional(s32[]{:T(128)} %convert_element_type.207, () %tuple.69, (bf16[2,1,1,2560,768]{4,3,2,1,0:T(8,128)(2,1)}, s32[]{:T(128)}, bf16[16,9,2560]{2,1,0:T(8,128)(2,1)S(1)}, bf16[2,1,1,2560,768]{4,3,2,1,0:T(8,128)(2,1)}, bf16[2,1,1,768,2560]{4,3,2,1,0:T(8,128)(2,1)}) %tuple.70), branch_computations={%region_8.8_spmd, %region_9.9_spmd} | conditional | flops 1699725312 | bytes 16369160 | solution.py:94
  402.5 2.9 fusion.14
  405.4 5.1 %fusion.11 = bf16[144,2560]{1,0:T(8,128)(2,1)S(1)} fusion(bf16[2,1,1,768,2560]{4,3,2,1,0:T(8,128)(2,1)} %get-tuple-element.443, s32[]{:T(128)} %get-tuple-element.440, bf16[144,2560]{1,0:T(8,128)(2,1)S(1)} %reshape.229, bf16[2,1,1,2560,768]{4,3,2,1,0:T(8,128)(2,1)} %get-tuple-element.442, f32[144,768]{1,0:T(8,128)S(1)} %fusion.14), kind=kOutput, calls=%fused_computation.10 | convolution fusion | flops 1133494272 | bytes 9782272 | tf_op jit(solution)/shard_map/while/body/eval_jaxpr/cond/branch_1_fun/dot_general | solution.py:46
  411.9 4.6 %all-to-all-start.1 = ((bf16[16,9,2560]{2,1,0:T(8,128)(2,1)}), bf16[16,9,2560]{2,1,0:T(8,128)(2,1)S(1)}, u32[]{:S(2)}, u32[]{:S(2)}) async-start(bf16[16,9,2560]{2,1,0:T(8,128)(2,1)} %reshape.245), calls=%async_computation.1 | async-start | bytes 2621440 | tf_op jit(solution)/shard_map/while/body/eval_jaxpr/all_to_all | solution.py:100
  418.4 28.9 %all-to-all-done.1 = bf16[16,9,2560]{2,1,0:T(8,128)(2,1)S(1)} async-done(((bf16[16,9,2560]{2,1,0:T(8,128)(2,1)}), bf16[16,9,2560]{2,1,0:T(8,128)(2,1)S(1)}, u32[]{:S(2)}, u32[]{:S(2)}) %all-to-all-start.1) | async-done | bytes 737312 | tf_op jit(solution)/shard_map/while/body/eval_jaxpr/all_to_all | solution.py:100
  448.1 4.4 collective-permute-done.1
  (171 shorter events, 44.3 us)
Async XLA Ops:
  5.3 37.0 %all-to-all-start = ((bf16[16,9,2560]{2,1,0:T(8,128)(2,1)}), bf16[16,9,2560]{2,1,0:T(8,128)(2,1)S(1)}, u32[]{:S(2)}, u32[]{:S(2)}) async-start(bf16[16,9,2560]{2,1,0:T(8,128)(2,1)} %reshape.244), calls=%async_computation | async-start | bytes 2621440 | tf_op jit(solution)/shard_map/while/body/eval_jaxpr/all_to_all | solution.py:93
  11.4 77.2 %collective-permute-start.2 = (bf16[16,2560]{1,0:T(8,128)(2,1)S(1)}, bf16[16,2560]{1,0:T(8,128)(2,1)S(1)}, u32[]{:S(2)}, u32[]{:S(2)}) collective-permute-start(bf16[16,2560]{1,0:T(8,128)(2,1)S(1)} %copy.43), channel_id=1, source_target_pairs={{16,0},{17,1},{18,2},{19,3},{20,4},{21,5},{22,6},{23,7},{24,8},{25... | collective-permute-start | bytes 245768 | tf_op jit(solution)/shard_map/while/body/eval_jaxpr/ppermute | solution.py:15
  42.3 16.7 %copy-start.1 = (bf16[2,1,2560,16]{2,3,1,0:T(8,128)(2,1)S(1)}, bf16[2,1,2560,16]{2,3,1,0:T(8,128)(2,1)}, u32[]{:S(2)}) copy-start(bf16[2,1,2560,16]{2,3,1,0:T(8,128)(2,1)} %get-tuple-element.725) | copy-start | bytes 491524 | tf_op jit(solution)/shard_map/while
  43.7 35.4 %all-to-all-start.1 = ((bf16[16,9,2560]{2,1,0:T(8,128)(2,1)}), bf16[16,9,2560]{2,1,0:T(8,128)(2,1)S(1)}, u32[]{:S(2)}, u32[]{:S(2)}) async-start(bf16[16,9,2560]{2,1,0:T(8,128)(2,1)} %reshape.245), calls=%async_computation.1 | async-start | bytes 2621440 | tf_op jit(solution)/shard_map/while/body/eval_jaxpr/all_to_all | solution.py:100
  48.3 31.3 %collective-permute-start = (bf16[16,2560]{1,0:T(8,128)(2,1)S(1)}, bf16[16,2560]{1,0:T(8,128)(2,1)S(1)}, u32[]{:S(2)}, u32[]{:S(2)}) collective-permute-start(bf16[16,2560]{1,0:T(8,128)(2,1)S(1)} %broadcast_select_fusion.6), channel_id=1, source_target_pairs={{16,0},{17,1},{18,2},{19,3},{20,4},{21,5},{22,6},{23,7},{24,8},{25... | collective-permute-start | bytes 245768 | tf_op jit(solution)/shard_map/while/body/eval_jaxpr/ppermute | solution.py:15
  79.8 11.2 %collective-permute-start.1 = (bf16[16,2560]{1,0:T(8,128)(2,1)S(1)}, bf16[16,2560]{1,0:T(8,128)(2,1)S(1)}, u32[]{:S(2)}, u32[]{:S(2)}) collective-permute-start(bf16[16,2560]{1,0:T(8,128)(2,1)S(1)} %get-tuple-element.674), channel_id=1, source_target_pairs={{0,16},{16,0},{1,17},{17,1},{2,18},{18,2},{3,19},{19,3},{4,20},{20... | collective-permute-start | bytes 245768 | tf_op jit(solution)/shard_map/while/body/eval_jaxpr/ppermute | solution.py:9
  95.4 35.9 %all-to-all-start = ((bf16[16,9,2560]{2,1,0:T(8,128)(2,1)}), bf16[16,9,2560]{2,1,0:T(8,128)(2,1)S(1)}, u32[]{:S(2)}, u32[]{:S(2)}) async-start(bf16[16,9,2560]{2,1,0:T(8,128)(2,1)} %reshape.244), calls=%async_computation | async-start | bytes 2621440 | tf_op jit(solution)/shard_map/while/body/eval_jaxpr/all_to_all | solution.py:93
  100.5 78.5 %collective-permute-start.2 = (bf16[16,2560]{1,0:T(8,128)(2,1)S(1)}, bf16[16,2560]{1,0:T(8,128)(2,1)S(1)}, u32[]{:S(2)}, u32[]{:S(2)}) collective-permute-start(bf16[16,2560]{1,0:T(8,128)(2,1)S(1)} %copy.43), channel_id=1, source_target_pairs={{16,0},{17,1},{18,2},{19,3},{20,4},{21,5},{22,6},{23,7},{24,8},{25... | collective-permute-start | bytes 245768 | tf_op jit(solution)/shard_map/while/body/eval_jaxpr/ppermute | solution.py:15
  139.6 9.7 %copy-start.1 = (bf16[2,1,2560,16]{2,3,1,0:T(8,128)(2,1)S(1)}, bf16[2,1,2560,16]{2,3,1,0:T(8,128)(2,1)}, u32[]{:S(2)}) copy-start(bf16[2,1,2560,16]{2,3,1,0:T(8,128)(2,1)} %get-tuple-element.725) | copy-start | bytes 491524 | tf_op jit(solution)/shard_map/while
  140.9 35.4 %all-to-all-start.1 = ((bf16[16,9,2560]{2,1,0:T(8,128)(2,1)}), bf16[16,9,2560]{2,1,0:T(8,128)(2,1)S(1)}, u32[]{:S(2)}, u32[]{:S(2)}) async-start(bf16[16,9,2560]{2,1,0:T(8,128)(2,1)} %reshape.245), calls=%async_computation.1 | async-start | bytes 2621440 | tf_op jit(solution)/shard_map/while/body/eval_jaxpr/all_to_all | solution.py:100
  145.6 31.3 %collective-permute-start = (bf16[16,2560]{1,0:T(8,128)(2,1)S(1)}, bf16[16,2560]{1,0:T(8,128)(2,1)S(1)}, u32[]{:S(2)}, u32[]{:S(2)}) collective-permute-start(bf16[16,2560]{1,0:T(8,128)(2,1)S(1)} %broadcast_select_fusion.6), channel_id=1, source_target_pairs={{16,0},{17,1},{18,2},{19,3},{20,4},{21,5},{22,6},{23,7},{24,8},{25... | collective-permute-start | bytes 245768 | tf_op jit(solution)/shard_map/while/body/eval_jaxpr/ppermute | solution.py:15
  177.1 4.5 collective-permute-start.1
  186.0 35.6 %all-to-all-start = ((bf16[16,9,2560]{2,1,0:T(8,128)(2,1)}), bf16[16,9,2560]{2,1,0:T(8,128)(2,1)S(1)}, u32[]{:S(2)}, u32[]{:S(2)}) async-start(bf16[16,9,2560]{2,1,0:T(8,128)(2,1)} %reshape.244), calls=%async_computation | async-start | bytes 2621440 | tf_op jit(solution)/shard_map/while/body/eval_jaxpr/all_to_all | solution.py:93
  190.8 78.5 %collective-permute-start.2 = (bf16[16,2560]{1,0:T(8,128)(2,1)S(1)}, bf16[16,2560]{1,0:T(8,128)(2,1)S(1)}, u32[]{:S(2)}, u32[]{:S(2)}) collective-permute-start(bf16[16,2560]{1,0:T(8,128)(2,1)S(1)} %copy.43), channel_id=1, source_target_pairs={{16,0},{17,1},{18,2},{19,3},{20,4},{21,5},{22,6},{23,7},{24,8},{25... | collective-permute-start | bytes 245768 | tf_op jit(solution)/shard_map/while/body/eval_jaxpr/ppermute | solution.py:15
  229.9 9.7 %copy-start.1 = (bf16[2,1,2560,16]{2,3,1,0:T(8,128)(2,1)S(1)}, bf16[2,1,2560,16]{2,3,1,0:T(8,128)(2,1)}, u32[]{:S(2)}) copy-start(bf16[2,1,2560,16]{2,3,1,0:T(8,128)(2,1)} %get-tuple-element.725) | copy-start | bytes 491524 | tf_op jit(solution)/shard_map/while
  231.3 35.4 %all-to-all-start.1 = ((bf16[16,9,2560]{2,1,0:T(8,128)(2,1)}), bf16[16,9,2560]{2,1,0:T(8,128)(2,1)S(1)}, u32[]{:S(2)}, u32[]{:S(2)}) async-start(bf16[16,9,2560]{2,1,0:T(8,128)(2,1)} %reshape.245), calls=%async_computation.1 | async-start | bytes 2621440 | tf_op jit(solution)/shard_map/while/body/eval_jaxpr/all_to_all | solution.py:100
  235.9 31.3 %collective-permute-start = (bf16[16,2560]{1,0:T(8,128)(2,1)S(1)}, bf16[16,2560]{1,0:T(8,128)(2,1)S(1)}, u32[]{:S(2)}, u32[]{:S(2)}) collective-permute-start(bf16[16,2560]{1,0:T(8,128)(2,1)S(1)} %broadcast_select_fusion.6), channel_id=1, source_target_pairs={{16,0},{17,1},{18,2},{19,3},{20,4},{21,5},{22,6},{23,7},{24,8},{25... | collective-permute-start | bytes 245768 | tf_op jit(solution)/shard_map/while/body/eval_jaxpr/ppermute | solution.py:15
  267.4 4.5 collective-permute-start.1
  276.3 35.6 %all-to-all-start = ((bf16[16,9,2560]{2,1,0:T(8,128)(2,1)}), bf16[16,9,2560]{2,1,0:T(8,128)(2,1)S(1)}, u32[]{:S(2)}, u32[]{:S(2)}) async-start(bf16[16,9,2560]{2,1,0:T(8,128)(2,1)} %reshape.244), calls=%async_computation | async-start | bytes 2621440 | tf_op jit(solution)/shard_map/while/body/eval_jaxpr/all_to_all | solution.py:93
  281.1 78.5 %collective-permute-start.2 = (bf16[16,2560]{1,0:T(8,128)(2,1)S(1)}, bf16[16,2560]{1,0:T(8,128)(2,1)S(1)}, u32[]{:S(2)}, u32[]{:S(2)}) collective-permute-start(bf16[16,2560]{1,0:T(8,128)(2,1)S(1)} %copy.43), channel_id=1, source_target_pairs={{16,0},{17,1},{18,2},{19,3},{20,4},{21,5},{22,6},{23,7},{24,8},{25... | collective-permute-start | bytes 245768 | tf_op jit(solution)/shard_map/while/body/eval_jaxpr/ppermute | solution.py:15
  320.2 9.7 %copy-start.1 = (bf16[2,1,2560,16]{2,3,1,0:T(8,128)(2,1)S(1)}, bf16[2,1,2560,16]{2,3,1,0:T(8,128)(2,1)}, u32[]{:S(2)}) copy-start(bf16[2,1,2560,16]{2,3,1,0:T(8,128)(2,1)} %get-tuple-element.725) | copy-start | bytes 491524 | tf_op jit(solution)/shard_map/while
  321.6 35.4 %all-to-all-start.1 = ((bf16[16,9,2560]{2,1,0:T(8,128)(2,1)}), bf16[16,9,2560]{2,1,0:T(8,128)(2,1)S(1)}, u32[]{:S(2)}, u32[]{:S(2)}) async-start(bf16[16,9,2560]{2,1,0:T(8,128)(2,1)} %reshape.245), calls=%async_computation.1 | async-start | bytes 2621440 | tf_op jit(solution)/shard_map/while/body/eval_jaxpr/all_to_all | solution.py:100
  326.2 31.3 %collective-permute-start = (bf16[16,2560]{1,0:T(8,128)(2,1)S(1)}, bf16[16,2560]{1,0:T(8,128)(2,1)S(1)}, u32[]{:S(2)}, u32[]{:S(2)}) collective-permute-start(bf16[16,2560]{1,0:T(8,128)(2,1)S(1)} %broadcast_select_fusion.6), channel_id=1, source_target_pairs={{16,0},{17,1},{18,2},{19,3},{20,4},{21,5},{22,6},{23,7},{24,8},{25... | collective-permute-start | bytes 245768 | tf_op jit(solution)/shard_map/while/body/eval_jaxpr/ppermute | solution.py:15
  357.7 4.5 collective-permute-start.1
  366.6 35.6 %all-to-all-start = ((bf16[16,9,2560]{2,1,0:T(8,128)(2,1)}), bf16[16,9,2560]{2,1,0:T(8,128)(2,1)S(1)}, u32[]{:S(2)}, u32[]{:S(2)}) async-start(bf16[16,9,2560]{2,1,0:T(8,128)(2,1)} %reshape.244), calls=%async_computation | async-start | bytes 2621440 | tf_op jit(solution)/shard_map/while/body/eval_jaxpr/all_to_all | solution.py:93
  371.4 76.7 %collective-permute-start.2 = (bf16[16,2560]{1,0:T(8,128)(2,1)S(1)}, bf16[16,2560]{1,0:T(8,128)(2,1)S(1)}, u32[]{:S(2)}, u32[]{:S(2)}) collective-permute-start(bf16[16,2560]{1,0:T(8,128)(2,1)S(1)} %copy.43), channel_id=1, source_target_pairs={{16,0},{17,1},{18,2},{19,3},{20,4},{21,5},{22,6},{23,7},{24,8},{25... | collective-permute-start | bytes 245768 | tf_op jit(solution)/shard_map/while/body/eval_jaxpr/ppermute | solution.py:15
  410.5 7.3 %copy-start.1 = (bf16[2,1,2560,16]{2,3,1,0:T(8,128)(2,1)S(1)}, bf16[2,1,2560,16]{2,3,1,0:T(8,128)(2,1)}, u32[]{:S(2)}) copy-start(bf16[2,1,2560,16]{2,3,1,0:T(8,128)(2,1)} %get-tuple-element.725) | copy-start | bytes 491524 | tf_op jit(solution)/shard_map/while
  411.9 35.4 %all-to-all-start.1 = ((bf16[16,9,2560]{2,1,0:T(8,128)(2,1)}), bf16[16,9,2560]{2,1,0:T(8,128)(2,1)S(1)}, u32[]{:S(2)}, u32[]{:S(2)}) async-start(bf16[16,9,2560]{2,1,0:T(8,128)(2,1)} %reshape.245), calls=%async_computation.1 | async-start | bytes 2621440 | tf_op jit(solution)/shard_map/while/body/eval_jaxpr/all_to_all | solution.py:100
  416.5 31.3 %collective-permute-start = (bf16[16,2560]{1,0:T(8,128)(2,1)S(1)}, bf16[16,2560]{1,0:T(8,128)(2,1)S(1)}, u32[]{:S(2)}, u32[]{:S(2)}) collective-permute-start(bf16[16,2560]{1,0:T(8,128)(2,1)S(1)} %broadcast_select_fusion.6), channel_id=1, source_target_pairs={{16,0},{17,1},{18,2},{19,3},{20,4},{21,5},{22,6},{23,7},{24,8},{25... | collective-permute-start | bytes 245768 | tf_op jit(solution)/shard_map/while/body/eval_jaxpr/ppermute | solution.py:15
  448.1 4.5 collective-permute-start.1
  452.6 0.6 copy-start
where the time goes:
time: 455 us; the launch traced here: 453 us
  waiting for transfers between devices  280 us (62%)
  starting transfers between devices  103 us (23%)
  matrix products  37 us (8%)
  local copies, waits for them, and re-layouts  27.4 us (6%)
  other arithmetic  4.87 us (1%)
    all_to_all x5, waiting for transfers between devices, layer(): lax.all_to_all(sending, 'expert', split_axis=0, concat_axis=0, tiled=True)  137 us
    all_to_all x5, waiting for transfers between devices, layer(): lax.all_to_all(answered, 'expert', split_axis=0, concat_axis=0, tiled=True)  128 us
    ppermute x10, starting transfers between devices, passed_along_2(): return lax.ppermute(block, axis, route)  39.8 us
    all_to_all x5, starting transfers between devices, layer(): lax.all_to_all(sending, 'expert', split_axis=0, concat_axis=0, tiled=True)  25.8 us
    all_to_all x5, starting transfers between devices, layer(): lax.all_to_all(answered, 'expert', split_axis=0, concat_axis=0, tiled=True)  23.2 us
    dot_general x4, matrix products, expert_rows(): jnp.dot(hidden, down_mat, preferred_element_type=jnp.float32)  20.4 us
    ppermute x5, waiting for transfers between devices, passed_along(): lax.ppermute(array, axis, [(i, (i + by) % size) for i in range(size)])  14.9 us
    ppermute x5, starting transfers between devices, passed_along(): lax.ppermute(array, axis, [(i, (i + by) % size) for i in range(size)])  14.3 us
  transfers between devices with their start and end apart: 25, of which 15 were waited for; matrix products, arithmetic and copies ran while one was open for 10% of the time, Pallas kernels for 0%

commit v1 on v0

v1 whole, which is shorter than its diff:
```python
import functools

import jax
import jax.numpy as jnp
from jax import lax
from jax.experimental import pallas as pl
from jax.experimental.pallas import tpu as pltpu
from jax.sharding import PartitionSpec as P

MESH = pl.DeviceIdType.MESH
F32 = jnp.float32
BF16 = jnp.bfloat16


def relay_kernel(
    sections, zs, parts,
    inp, gain, router, routes, wg_hbm, wu_hbm, wd_hbm,
    out,
    wg, wu, wd, xin, xout, g, hid, gate_col, p, rc, qs, own, rx, ss, rz,
    w_sem, xin_s, xin_r, feed_s, ag_s, ag_r, c_s, c_r, x_s, x_r, z_s, z_r,
):
    slab = inp.shape[1]
    width = inp.shape[2]
    hidden = wg.shape[2]
    experts = 4 * zs
    half = 2 * zs * slab
    quarter = zs * slab
    piece = width // parts
    moments = 2 * sections

    sec = lax.axis_index("section")
    me = lax.axis_index("expert")
    z = lax.div(me, 4)
    x = lax.rem(lax.div(me, 2), 2)
    c = lax.rem(me, 2)
    x_dev = z * 4 + (1 - x) * 2 + c
    c_dev = z * 4 + x * 2 + (1 - c)
    z_at = [lax.rem(z + k, zs) for k in range(1, zs)]
    z_dev = [zk * 4 + x * 2 + c for zk in z_at]

    def weight_copies(loop_at):
        return [
            pltpu.make_async_copy(src.at[loop_at, 0, 0], dst.at[loop_at], w_sem.at[loop_at, k])
            for k, (src, dst) in enumerate(((wg_hbm, wg), (wu_hbm, wu), (wd_hbm, wd)))
        ]

    for loop_at in range(2):
        for copy in weight_copies(loop_at):
            copy.start()

    barrier = pltpu.get_barrier_semaphore()
    for dev in z_dev + [x_dev, c_dev]:
        pl.semaphore_signal(barrier, inc=1, device_id=(sec, dev), device_id_type=MESH)
    for k in range(1, sections):
        pl.semaphore_signal(
            barrier, inc=1, device_id=(lax.rem(sec + k, sections), me), device_id_type=MESH
        )
    pl.semaphore_wait(barrier, zs + 1 + sections - 1)

    def remote(src, dst, s_sem, r_sem, section_to, dev):
        return pltpu.make_async_remote_copy(
            src_ref=src, dst_ref=dst, send_sem=s_sem, recv_sem=r_sem,
            device_id=(section_to, dev), device_id_type=MESH,
        )

    feed = remote(inp.at[0], xin.at[sec], feed_s.at[0], xin_r.at[sec], sec * 0, me)

    @pl.when(sec > 0)
    def _():
        feed.start()

    @pl.when(sec == 0)
    def _():
        xin[0] = inp[0]

    def slab_rows(ref, q):
        return ref.at[pl.ds(pl.multiple_of(q * slab, slab), slab), :]

    def spread(q, k, dev):
        return remote(slab_rows(g, q), slab_rows(g, q), ag_s.at[k], ag_r.at[q], sec, dev)

    def q_of(cc, xx, zz):
        return cc * (2 * zs) + xx * zs + zz

    last = lax.div(sec, sections - 1)

    def hand_over(j):
        upper = lax.div(j, sections)
        to = (1 - last) * (sec + 1) + last * upper * (j - sections)
        slot = j + last * (sections * (1 - upper) + upper * (2 * sections - j))
        return remote(xout.at[j], xin.at[slot], xin_s.at[j], xin_r.at[slot], to, me)

    def step(j, carry):
        loop_at = lax.div(j, sections)
        micro_at = lax.rem(j, sections)

        @pl.when(sec + j > 0)
        def _():
            remote(xout.at[0], xin.at[j], xin_s.at[0], xin_r.at[j], sec, x_dev).wait_recv()

        wide = xin[j].astype(F32)
        scale = lax.rsqrt(jnp.sum(wide * wide, axis=-1, keepdims=True) * (1.0 / width) + 1e-06)
        q_me = q_of(c, x, z)
        g[pl.ds(pl.multiple_of(q_me * slab, slab), slab), :] = (
            wide * scale * gain[loop_at]
        ).astype(BF16)

        sent = []

        def launch(q, dev):
            copy = spread(q, len(sent), dev)
            copy.start()
            sent.append(copy)

        def arrive(q):
            spread(q, 0, x_dev).wait_recv()

        for dev in z_dev:
            launch(q_me, dev)
        launch(q_me, x_dev)
        launch(q_me, c_dev)
        near = [0, zs - 2] + list(range(1, zs - 2))
        for k in near:
            q = q_of(c, x, z_at[k])
            arrive(q)
            launch(q, x_dev)
            launch(q, c_dev)
        for zz in [z] + [z_at[k] for k in near]:
            q = q_of(c, 1 - x, zz)
            arrive(q)
            launch(q, c_dev)
        for xx in (x, 1 - x):
            for zz in [z] + [z_at[k] for k in near]:
                arrive(q_of(1 - c, xx, zz))

        @pl.when(micro_at == 0)
        def _():
            for copy in weight_copies(loop_at):
                copy.wait()

        scores = jnp.dot(g[...], router[loop_at, 0], preferred_element_type=F32)
        lanes = lax.broadcasted_iota(jnp.int32, scores.shape, 1)
        rows = []
        for cc in range(2):
            for xx in range(2):
                for zz in range(zs):
                    i = zz * 4 + xx * 2 + cc
                    rows.append(routes[loop_at, 0, micro_at, i * slab:(i + 1) * slab, :])
        chosen = jnp.concatenate(rows, axis=0)
        hit = chosen[:, 0:1] == lanes
        for k in range(1, routes.shape[4]):
            hit = hit | (chosen[:, k:k + 1] == lanes)
        sig = jnp.where(hit, jax.nn.sigmoid(scores), 0.0)
        mine = jnp.sum(jnp.where(lanes == me, sig, 0.0), axis=1, keepdims=True)
        gate_col[...] = mine / jnp.sum(sig, axis=1, keepdims=True)

        cut = 256
        for h in range(hidden // cut):
            cols = slice(h * cut, (h + 1) * cut)
            gate = jnp.dot(g[...], wg[loop_at, :, cols], preferred_element_type=F32)
            up = jnp.dot(g[...], wu[loop_at, :, cols], preferred_element_type=F32)
            hid[:, cols] = (gate * jax.nn.sigmoid(gate) * up).astype(BF16)

        for copy in sent:
            copy.wait_send()

        def block(ref, start, count, n):
            first = start if isinstance(start, int) else pl.multiple_of(start, slab)
            return ref.at[pl.ds(first, count), pl.ds(n * piece, piece)]

        c_sent, x_sent, z_sent = [], [], []
        for n in range(parts):
            cols = slice(n * piece, (n + 1) * piece)
            down = jnp.dot(hid[...], wd[loop_at, :, cols], preferred_element_type=F32)
            p[:, cols] = (down * gate_col[...]).astype(BF16)
            copy = remote(
                block(p, (1 - c) * half, half, n), block(rc, 0, half, n),
                c_s.at[n], c_r.at[n], sec, c_dev,
            )
            copy.start()
            c_sent.append(copy)
        for n in range(parts):
            c_sent[n].wait_recv()
            away = block(p, c * half + (1 - x) * quarter, quarter, n)[...].astype(F32)
            qs[:, n * piece:(n + 1) * piece] = (
                away + block(rc, (1 - x) * quarter, quarter, n)[...].astype(F32)
            ).astype(BF16)
            copy = remote(
                block(qs, 0, quarter, n), block(rx, 0, quarter, n),
                x_s.at[n], x_r.at[n], sec, x_dev,
            )
            copy.start()
            x_sent.append(copy)
            own[:, n * piece:(n + 1) * piece] = (
                block(p, c * half + x * quarter, quarter, n)[...].astype(F32)
                + block(rc, x * quarter, quarter, n)[...].astype(F32)
            )
        for n in range(parts):
            cols = slice(n * piece, (n + 1) * piece)
            x_sent[n].wait_recv()
            own[:, cols] = own[:, cols] + rx[:, cols].astype(F32)
            ss[:, cols] = own[:, cols].astype(BF16)
            for k in range(zs - 1):
                copy = remote(
                    block(ss, z_at[k] * slab, slab, n), block(rz, k * slab, slab, n),
                    z_s.at[k, n], z_r.at[k, n], sec, z_dev[k],
                )
                copy.start()
                z_sent.append(copy)
        for n in range(parts):
            cols = slice(n * piece, (n + 1) * piece)
            total = block(own, z * slab, slab, n)[...]
            for k in range(zs - 1):
                z_sent[n * (zs - 1) + k].wait_recv()
                total = total + rz[k * slab:(k + 1) * slab, cols].astype(F32)
            xout[j, :, cols] = (xin[j, :, cols].astype(F32) + total).astype(BF16)

        stays = sec + j == (sections - 1) + (moments - 1)

        @pl.when(jnp.logical_not(stays))
        def _():
            hand_over(j).start()

        @pl.when(stays)
        def _():
            xin[moments] = xout[j]

        for copy in c_sent + x_sent + z_sent:
            copy.wait_send()
        return carry

    lax.fori_loop(0, moments, step, 0)

    @pl.when(sec > 0)
    def _():
        feed.wait_send()

    def drain(j, carry):
        @pl.when(sec + j < (sections - 1) + (moments - 1))
        def _():
            hand_over(j).wait_send()
        return carry

    lax.fori_loop(0, moments, drain, 0)

    @pl.when(sec < sections - 1)
    def _():
        remote(
            xout.at[0], xin.at[moments], xin_s.at[0], xin_r.at[moments], sec, x_dev
        ).wait_recv()

    out[0] = xin[moments]


def per_device(inputs, norm_gain, router, w_gate, w_up, w_down, routes):
    sections = lax.axis_size("section")
    experts = lax.axis_size("expert")
    zs = experts // 4
    slab = inputs.shape[1]
    width = inputs.shape[2]
    hidden = w_gate.shape[4]
    tokens = experts * slab
    parts = 5
    moments = 2 * sections
    vmem = pl.BlockSpec(memory_space=pltpu.VMEM)
    anywhere = pl.BlockSpec(memory_space=pl.ANY)
    dma = pltpu.SemaphoreType.DMA
    return pl.pallas_call(
        functools.partial(relay_kernel, sections, zs, parts),
        out_shape=jax.ShapeDtypeStruct(inputs.shape, inputs.dtype),
        in_specs=[vmem] * 4 + [anywhere] * 3,
        out_specs=vmem,
        scratch_shapes=[
            pltpu.VMEM((2, width, hidden), BF16),
            pltpu.VMEM((2, width, hidden), BF16),
            pltpu.VMEM((2, hidden, width), BF16),
            pltpu.VMEM((moments + 1, slab, width), BF16),
            pltpu.VMEM((moments, slab, width), BF16),
            pltpu.VMEM((tokens, width), BF16),
            pltpu.VMEM((tokens, hidden), BF16),
            pltpu.VMEM((tokens, 1), F32),
            pltpu.VMEM((tokens, width), BF16),
            pltpu.VMEM((tokens // 2, width), BF16),
            pltpu.VMEM((tokens // 4, width), BF16),
            pltpu.VMEM((tokens // 4, width), F32),
            pltpu.VMEM((tokens // 4, width), BF16),
            pltpu.VMEM((tokens // 4, width), BF16),
            pltpu.VMEM(((zs - 1) * slab, width), BF16),
            dma((2, 3)),
            dma((moments,)),
            dma((moments + 1,)),
            dma((1,)),
            dma((experts - 1,)),
            dma((experts,)),
            dma((parts,)),
            dma((parts,)),
            dma((parts,)),
            dma((parts,)),
            dma((zs - 1, parts)),
            dma((zs - 1, parts)),
        ],
        compiler_params=pltpu.CompilerParams(
            collective_id=0, has_side_effects=True, vmem_limit_bytes=56 * 1024 * 1024
        ),
    )(inputs, norm_gain, router, routes, w_gate, w_up, w_down)


def solution(mesh):
    return jax.shard_map(
        per_device,
        mesh=mesh,
        in_specs=(
            P("section", "expert", None),
            P(None, "section", None),
            P(None, "section", None, None),
            P(None, "section", "expert", None, None),
            P(None, "section", "expert", None, None),
            P(None, "section", "expert", None, None),
            P(None, "section", None, None, None),
        ),
        out_specs=P("section", "expert", None),
        check_vma=False,
    )
```

time: 455 us -> 178 us (0.39)
  waiting for transfers between devices: 280 us -> 0 us
  Pallas kernels: 0 us -> 171 us
  starting transfers between devices: 103 us -> 0 us
  matrix products: 37 us -> 0 us
  local copies, waits for them, and re-layouts: 27.4 us -> 5.71 us
  other arithmetic: 4.87 us -> 0 us
    all_to_all x10 -> x0, waiting for transfers between devices: 265 us -> none  [the longest x5 137 us: layer(): lax.all_to_all(sending, 'expert', split_axis=0, concat_axis=0, tiled=True)]
    pallas_call x0 -> x1, Pallas kernels: none -> 171 us  [per_device(): pl.pallas_call(functools.partial(relay_kernel, sections, zs, parts), out_...]
    ppermute x15 -> x0, starting transfers between devices: 54.1 us -> none  [the longest x10 39.8 us: passed_along_2(): return lax.ppermute(block, axis, route)]
    all_to_all x10 -> x0, starting transfers between devices: 49 us -> none  [the longest x5 25.8 us: layer(): lax.all_to_all(sending, 'expert', split_axis=0, concat_axis=0, tiled=True)]
    dot_general x28 -> x0, matrix products: 37 us -> none  [the longest x4 20.4 us: expert_rows(): jnp.dot(hidden, down_mat, preferred_element_type=jnp.float32)]
    reshape x29 -> x0, local copies, waits for them, and re-layouts: 17.3 us -> none  [the longest x5 6.79 us: layer(): sending = sending.reshape(experts, capacity, feature)]
    ppermute x15 -> x0, waiting for transfers between devices: 14.9 us -> none  [the longest x5 14.9 us: passed_along(): lax.ppermute(array, axis, [(i, (i + by) % size) for i in range(size)])]
    dynamic_slice x20 -> x0, local copies, waits for them, and re-layouts: 7.98 us -> none  [the longest x15 4.29 us: layer(): lax.dynamic_slice_in_dim(routes_now, owner_at * slab_rows, slab_rows, 0)]
  transfers between devices with their start and end apart: 25 -> 0, of which waited for: 15 -> 0; matrix products, arithmetic and copies ran while one was open for 10% -> 0% of each run, Pallas kernels for 0% -> 0%
where the time goes in v1:
time: 178 us; the launch traced here: 176 us
  Pallas kernels  171 us (96%)
  local copies, waits for them, and re-layouts  5.71 us (3%)
    pallas_call x1, Pallas kernels, per_device(): pl.pallas_call(functools.partial(relay_kernel, sections, zs, parts), out_...  171 us
    unnamed x3, local copies, waits for them, and re-layouts  5.71 us

profile of v1, /device:TPU:20, one launch (start us, length us, event | category | flops | bytes accessed | tf_op | source)
XLA Modules:
  0.0 176.4 jit_solution(15724979409977477411)
XLA Ops:
  0.0 1.8 %copy.9.routes = s32[2,1,2,256,6]{4,3,2,1,0:T(8,128)} copy(s32[2,1,2,256,6]{3,2,4,1,0:T(2,128)} %param.13) | data formatting | bytes 49152 | tf_op args[6]
  1.8 2.4 %copy.8.router = bf16[2,1,2560,16]{3,2,1,0:T(8,128)(2,1)} copy(bf16[2,1,2560,16]{2,3,1,0:T(8,128)(2,1)} %param.9) | data formatting | bytes 327680 | tf_op args[2]
  4.2 170.6 %shard_map.73 = bf16[1,16,2560]{2,1,0:T(8,128)(2,1)} custom-call(bf16[1,16,2560]{2,1,0:T(8,128)(2,1)} %inp.1, f32[2,1,2560]{2,1,0:T(1,128)} %gain.1, bf16[2,1,2560,16]{3,2,1,0:T(8,128)(2,1)} %copy.8.router, s32[2,1,2,256,6]{4,3,2,1,0:T(8,128)} %copy.9.routes, bf16[2,1,1,2560,768]{4,3,2,1,0:T(8,128)(2,1)} %wg_hbm.1, bf16[2,1,1,2560,768]{4,3,2,1,0:T(8,128)(2,1)} %wu_hbm.1, ...), custom_call_target="tpu_custom_call" | custom-call | tf_op jit(solution)/shard_map/pallas_call | solution.py:268
  174.8 1.5 copy.11
